TPU v7x, 32 devices: a whole 2x2x4 slice. The times are simulated.
32 devices in a mesh: chan: 8 (over z, core), ctx: 4 (over y, x).
Axes of the slice: x: 2, y: 2, z: 4, core: 2. Of those that a mesh axis runs over, the one named last changes fastest.
Arguments:
- saved_input: float32 [2, 128, 32768], P(None, 'chan', 'ctx'), may hold values from -6 to 6
- out_grad: float32 [2, 128, 32768], P(None, 'chan', 'ctx'), may hold values from -6 to 6
- filters: float32 [2, 32768], P(None, 'ctx'), may hold values from -0.03125 to 0.03125
Outputs:
- input_grad: bfloat16 [2, 128, 32768], P(None, 'chan', 'ctx')
- filter_grad: float32 [2, 32768], P(None, 'ctx')
All inputs are finite; a program needn't handle non-finite values.
Results may differ from a plain program's by a relative error of at most 0.001.
Values sent between devices are 32-bit elements; how exact they have to be, the bound alone decides.
A program may use at most 128 MiB of HBM per device.

v0:
```python
import math

import jax
import jax.numpy as jnp
from jax import lax
from jax.sharding import PartitionSpec as P

RADIX = 32


precise = lax.Precision.HIGHEST


def dft_tables(length, sign_value):
    positions = jnp.arange(length, dtype=jnp.int32)
    phases = positions[:, None] * positions[None, :] % length
    angles = 2.0 * math.pi / length * phases.astype(jnp.float32)
    return (jnp.cos(angles), sign_value * jnp.sin(angles))


def rotate(values, angles):
    cosine = jnp.cos(angles)
    sine_part = jnp.sin(angles)
    real_part = values[0] * cosine - values[1] * sine_part
    imag_part = values[0] * sine_part + values[1] * cosine
    return jnp.stack([real_part, imag_part])


def inner_angles(first_factor, second_factor, sign_value):
    period = first_factor * second_factor
    lefts = jnp.arange(first_factor, dtype=jnp.int32)[:, None]
    rights = jnp.arange(second_factor, dtype=jnp.int32)[None, :]
    phases = lefts * rights % period
    return sign_value * 2.0 * math.pi / period * phases.astype(jnp.float32)


def slot_frequency(slots, devices):
    owner = slots // 2
    parity = slots % 2
    return jnp.where(
        owner == 0, parity * devices, jnp.where(parity == 0, owner, 2 * devices - owner)
    )


def paired_angles(device, devices, tokens, sign_value):
    frequency = slot_frequency(2 * device + jnp.arange(2, dtype=jnp.int32), devices)[:, None]
    offsets = jnp.arange(tokens, dtype=jnp.int32)[None, :]
    period = 2 * devices * tokens
    phases = offsets * frequency % period
    return sign_value * 2.0 * math.pi / period * phases.astype(jnp.float32)


def complex_apply(form, cosine, sine_part, real_part, imag_part):
    new_real = jnp.einsum(form, real_part, cosine, precision=precise) - jnp.einsum(
        form, imag_part, sine_part, precision=precise
    )
    new_imag = jnp.einsum(form, real_part, sine_part, precision=precise) + jnp.einsum(
        form, imag_part, cosine, precision=precise
    )
    return jnp.stack([new_real, new_imag])


def local_forward(values, first_factor, second_factor):
    cosine, sine_part = dft_tables(first_factor, -1.0)
    sectioned = complex_apply("rpab,ak->rpbk", cosine, sine_part, values[0], values[1])
    sectioned = rotate(sectioned, inner_angles(first_factor, second_factor, -1.0).T)
    cosine, sine_part = dft_tables(second_factor, -1.0)
    return complex_apply("rpbk,bm->rpkm", cosine, sine_part, sectioned[0], sectioned[1])


def local_inverse(values, first_factor, second_factor):
    cosine, sine_part = dft_tables(second_factor, 1.0)
    sectioned = complex_apply("rpkm,mb->rpkb", cosine, sine_part, values[0], values[1])
    sectioned = rotate(sectioned, inner_angles(first_factor, second_factor, 1.0))
    cosine, sine_part = dft_tables(first_factor, 1.0)
    result = complex_apply("rpkb,ka->rpba", cosine, sine_part, sectioned[0], sectioned[1])
    return jnp.swapaxes(result, -1, -2)


def paired_kernel(devices):
    blocks = jnp.arange(devices, dtype=jnp.int32)[:, None]
    frequencies = slot_frequency(jnp.arange(2 * devices, dtype=jnp.int32), devices)[None, :]
    angles = math.pi / devices * (blocks * frequencies % (2 * devices)).astype(jnp.float32)
    cosine = jnp.cos(angles)
    sine_part = jnp.sin(angles)
    return jnp.stack(
        [jnp.stack([cosine, -sine_part], axis=1), jnp.stack([sine_part, cosine], axis=1)], axis=0
    )


def paired_back_kernel(devices):
    frequencies = slot_frequency(jnp.arange(2 * devices, dtype=jnp.int32), devices)[:, None]
    blocks = jnp.arange(devices, dtype=jnp.int32)[None, :]
    angles = math.pi / devices * (frequencies * blocks % (2 * devices)).astype(jnp.float32)
    cosine = jnp.cos(angles)
    sine_part = jnp.sin(angles)
    return jnp.stack(
        [jnp.stack([cosine, sine_part], axis=1), jnp.stack([-sine_part, cosine], axis=1)], axis=0
    )


def mirror_spectra(values, device, first_factor):
    flipped = jnp.flip(values, axis=(3, 4))
    swapped = flipped[:, :, ::-1]
    lowest = flipped[:, :, 0]
    moved = jnp.concatenate(
        [jnp.roll(lowest[:, :, first_factor - 1 :], 1, axis=3), lowest[:, :, : first_factor - 1]],
        axis=2,
    )
    own = jnp.stack([moved, flipped[:, :, 1]], axis=2)
    return jnp.where(device == 0, own, swapped)


def local(saved_input, out_grad, filters):
    batch_size, channels, tokens = saved_input.shape
    groups = filters.shape[0]
    devices = lax.axis_size("ctx")
    device = lax.axis_index("ctx")
    first_factor = RADIX
    second_factor = tokens // RADIX
    row_count = batch_size * channels
    half_rows = row_count // 2
    real_rows = jnp.concatenate([saved_input.reshape(row_count, tokens), filters[0::2]], axis=0)
    imag_rows = jnp.concatenate([out_grad.reshape(row_count, tokens), filters[1::2]], axis=0)
    packed_rows = row_count + groups // 2
    packed = jnp.stack([real_rows, imag_rows]).reshape(2, packed_rows, 1, tokens)
    columns = lax.all_to_all(packed, "ctx", split_axis=3, concat_axis=2, tiled=True)
    mixed_part = jnp.einsum("cpxj,cxdu->dpuj", columns, paired_kernel(devices), precision=precise)
    values = lax.all_to_all(mixed_part, "ctx", split_axis=2, concat_axis=3, tiled=True)
    forward_turns = paired_angles(device, devices, tokens, -1.0)
    inverse_turns = paired_angles(device, devices, tokens, 1.0)
    values = rotate(values, forward_turns)
    rows_now = values.shape[1]
    values = local_forward(
        values.reshape(2, rows_now, 2, first_factor, second_factor), first_factor, second_factor
    )
    mirror = mirror_spectra(values, device, first_factor)
    first_part = jnp.stack([(values[0] + mirror[0]) * 0.5, (values[1] - mirror[1]) * 0.5])
    second_part = jnp.stack([(values[1] + mirror[1]) * 0.5, (mirror[0] - values[0]) * 0.5])
    filter_both = jnp.stack([first_part[:, row_count:], second_part[:, row_count:]], axis=2)
    filter_both = filter_both.reshape(2, groups, 2, first_factor, second_factor)
    values = jnp.concatenate(
        [first_part[:, :row_count], second_part[:, :row_count], filter_both], axis=1
    )
    per_filter = channels // groups
    spectrum_shape = (2, batch_size, per_filter, groups, 2, first_factor, second_factor)
    in_spec = values[:, :row_count].reshape(spectrum_shape)
    grad_spec = values[:, row_count : 2 * row_count].reshape(spectrum_shape)
    filter_spec = values[:, 2 * row_count :].reshape(
        2, 1, 1, groups, 2, first_factor, second_factor
    )
    input_spec = jnp.stack(
        [
            filter_spec[0] * grad_spec[0] + filter_spec[1] * grad_spec[1],
            filter_spec[0] * grad_spec[1] - filter_spec[1] * grad_spec[0],
        ]
    ).reshape(2, row_count, 2, first_factor, second_factor)
    filter_part = jnp.stack(
        [
            jnp.sum(in_spec[0] * grad_spec[0] + in_spec[1] * grad_spec[1], axis=(0, 1)),
            jnp.sum(in_spec[0] * grad_spec[1] - in_spec[1] * grad_spec[0], axis=(0, 1)),
        ]
    )
    filter_part = lax.psum(filter_part, "chan")
    joined = jnp.concatenate([input_spec, filter_part], axis=1)
    left_rows = jnp.concatenate([joined[:, :half_rows], joined[:, row_count::2]], axis=1)
    right_rows = jnp.concatenate(
        [joined[:, half_rows:row_count], joined[:, row_count + 1 :: 2]], axis=1
    )
    joined = jnp.stack([left_rows[0] - right_rows[1], left_rows[1] + right_rows[0]])
    rows_back = joined.shape[1]
    values = local_inverse(joined, first_factor, second_factor).reshape(2, rows_back, 2, tokens)
    values = rotate(values, inverse_turns)
    columns = lax.all_to_all(values, "ctx", split_axis=3, concat_axis=2, tiled=True)
    restored = jnp.einsum(
        "cpuj,cudx->dpxj", columns, paired_back_kernel(devices), precision=precise
    )
    both_parts = lax.all_to_all(restored, "ctx", split_axis=2, concat_axis=3, tiled=True).reshape(
        2, rows_back, tokens
    )
    input_rows = jnp.concatenate([both_parts[0, :half_rows], both_parts[1, :half_rows]], axis=0)
    filter_rows = jnp.stack([both_parts[0, half_rows:], both_parts[1, half_rows:]], axis=1).reshape(
        groups, tokens
    )
    signal = jnp.concatenate([input_rows, filter_rows], axis=0)
    signal = signal * (1.0 / (2 * devices * tokens))
    input_grad = signal[:row_count].reshape(batch_size, channels, tokens).astype(jnp.bfloat16)
    filter_grad = signal[row_count:]
    norm_factor = float(tokens * devices * batch_size * per_filter * lax.axis_size("chan")) ** (
        -0.5
    )
    return (input_grad, filter_grad * norm_factor)


def solution(mesh):
    placed = (P(None, "chan", "ctx"), P(None, "chan", "ctx"), P(None, "ctx"))
    return jax.shard_map(
        local,
        mesh=mesh,
        in_specs=placed,
        out_specs=(P(None, "chan", "ctx"), P(None, "ctx")),
        check_vma=False,
    )
```

profile of v0, /device:TPU:0, one launch (start us, length us, event | category | flops | bytes accessed | tf_op | source)
XLA Modules:
  0.0 518.1 jit_solution(7195402960022230788)
XLA Ops:
  10.1 8.0 %copy.74 = f32[2,33,1,8192]{1,0,2,3:T(2,128)} copy(f32[2,33,1,8192]{3,1,0,2:T(8,128)S(1)} %maximum_bitcast_fusion) | data formatting | bytes 4325376 | tf_op jit(solution)/shard_map/reshape | solution.py:126
  18.1 17.0 %reshape.643 = f32[4,1,135168]{2,1,0:T(1,128)} reshape(f32[8192,1,2,33]{3,2,1,0:T(2,128)} %bitcast.199) | data formatting | bytes 4325376
  35.1 5.4 %all-to-all-start = ((f32[4,1,135168]{2,1,0:T(1,128)}), f32[4,1,135168]{2,1,0:T(1,128)S(1)}, u32[]{:S(2)}, u32[]{:S(2)}) async-start(f32[4,1,135168]{2,1,0:T(1,128)} %reshape.643), calls=%async_computation | async-start | bytes 4325376 | tf_op jit(solution)/shard_map/all_to_all | solution.py:127
  40.6 25.4 %all-to-all-done = f32[4,1,135168]{2,1,0:T(1,128)S(1)} async-done(((f32[4,1,135168]{2,1,0:T(1,128)}), f32[4,1,135168]{2,1,0:T(1,128)S(1)}, u32[]{:S(2)}, u32[]{:S(2)}) %all-to-all-start) | async-done | bytes 2162720 | tf_op jit(solution)/shard_map/all_to_all | solution.py:127
  67.9 7.4 %reduce = f32[4,135168]{1,0:T(4,128)S(1)} reduce(f32[4,1,135168]{2,1,0:T(1,128)} %copy-done.4, f32[]{:T(128)} %broadcast.1003), dimensions={1}, to_apply=%all_to_all.40.reduce_sub_computation | reduce | bytes 4325380 | tf_op jit(solution)/shard_map/all_to_all | solution.py:127
  75.3 17.6 %reshape.644 = f32[8192,1,2,33]{3,2,1,0:T(2,128)} reshape(f32[4,135168]{1,0:T(4,128)S(1)} %reduce) | data formatting | bytes 4325376
  92.9 10.6 %copy.97 = f32[2,33,4,2048]{3,2,0,1:T(4,128)S(1)} copy(f32[2,33,4,2048]{1,0,3,2:T(2,128)} %bitcast.198) | data formatting | bytes 4325376 | tf_op jit(solution)/shard_map/all_to_all | solution.py:127
  103.6 4.4 convolution_bitcast_fusion
  108.0 5.4 %copy.76 = f32[2,33,8,2048]{3,0,1,2:T(2,128)} copy(f32[2,33,8,2048]{3,2,1,0:T(8,128)S(1)} %convolution_bitcast_fusion) | data formatting | bytes 8650752 | tf_op jit(solution)/shard_map/cpxj,cxdu->dpuj/transpose | solution.py:128
  113.4 4.9 all-to-all-start.1
  120.6 46.0 %all-to-all-done.1 = f32[2,33,8,2048]{3,0,1,2:T(2,128)} async-done(((f32[2,33,8,2048]{3,0,1,2:T(2,128)}), f32[2,33,8,2048]{3,0,1,2:T(2,128)}, u32[]{:S(2)}, u32[]{:S(2)}) %all-to-all-start.1) | async-done | bytes 4325408 | tf_op jit(solution)/shard_map/all_to_all | solution.py:129
  166.6 9.5 %fusion.201 = (f32[1,33,2,4,2048]{4,0,1,2,3:T(1,128)S(1)}, f32[1,33,2,4,2048]{4,0,1,2,3:T(1,128)}) fusion(f32[2,33,2,4,2048]{4,0,1,2,3:T(2,128)} %bitcast.21), kind=kLoop, calls=%fused_computation.288 | loop fusion | bytes 8650752 | tf_op jit(solution)/shard_map/slice | solution.py:24
  181.5 4.4 copy.78
  185.9 3.6 squeeze.19
  189.5 4.0 fusion.19
  215.2 5.3 %slice.166 = f32[2,33,1,32,256]{4,3,1,0,2:T(8,128)} reverse(f32[2,33,1,32,256]{4,3,1,0,2:T(8,128)} %get-tuple-element.17), dimensions={3,4} | reverse | bytes 4325376 | tf_op jit(solution)/shard_map/slice | solution.py:105
  222.7 4.1 pad_maximum_fusion
  226.8 5.3 %slice.171 = f32[2,33,1,32,256]{4,3,2,1,0:T(8,128)} reverse(f32[2,33,1,32,256]{4,3,2,1,0:T(8,128)} %get-tuple-element.18), dimensions={3,4} | reverse | bytes 4325376 | tf_op jit(solution)/shard_map/slice | solution.py:110
  232.1 9.8 %rev.5 = f32[2,33,2,32,256]{4,3,2,1,0:T(8,128)} reverse(f32[2,33,2,32,256]{4,3,2,1,0:T(8,128)} %pad_maximum_fusion), dimensions={2,3,4} | reverse | bytes 8650752 | tf_op jit(solution)/shard_map/rev | solution.py:104
  244.8 5.2 %maximum_select_fusion = f32[2,33,2,32,256]{4,3,2,1,0:T(8,128)} fusion(f32[2,33,2,32,256]{4,3,2,1,0:T(8,128)S(1)} %copy-done.3, f32[2,33,1,32,256]{4,3,2,1,0:T(8,128)} %slice.171, f32[2,33,1,32,256]{4,3,2,1,0:T(8,128)S(1)} %maximum_bitcast_fusion.2, pred[]{:T(512)S(6)} %eq.97), kind=kLoop, calls=%fused_computation.5 | loop fusion | flops 2162688 | bytes 12976129 | tf_op jit(solution)/shard_map/jit(_where)/select_n | solution.py:111
  250.0 6.4 %fusion.12 = (f32[1,33,2,32,256]{4,3,2,1,0:T(8,128)}, f32[1,33,2,32,256]{4,3,2,0,1:T(8,128)S(1)}, f32[1,33,2,32,256]{4,3,2,1,0:T(8,128)S(1)}, f32[1,33,2,32,256]...) fusion(f32[33,2,32,256]{3,2,1,0:T(8,128)S(1)} %copy-done.2, ...), kind=kLoop, calls=%fused_computation.61 | loop fusion | flops 4325376 | bytes 21626880 | tf_op jit(solution)/shard_map/stack | solution.py:139
  260.3 6.4 %multiply_add_fusion.2 = (f32[1,32,2,32,256]{4,3,2,1,0:T(8,128)}, f32[1,32,2,32,256]{4,3,2,1,0:T(8,128)S(1)}, f32[1,32,2,32,256]{4,3,2,1,0:T(8,128)}, f32[1,32,2,32,256]{4,3,2,1,0:T(8,128)}) fusion(f32[1,33,2,32,256]{4,3,2,1,0:T(8,128)S(1)} %get-tuple-element.8, f32[1,33,2,32,256]{4,3,2,1,0:T(8,128)S(1)} %get-tuple-element.14, ...), kind=kLoop, calls=%fused_computation.34 | loop fusion | flops 6291456 | bytes 20971520 | tf_op jit(solution)/shard_map/add | solution.py:160
  271.1 54.3 %all-reduce.2.cloned.1.call-done = f32[2,2,2,32,256]{4,3,2,1,0:T(8,128)} async-done(((f32[2,2,2,32,256]{4,3,2,1,0:T(8,128)}), f32[2,2,2,32,256]{4,3,2,1,0:T(8,128)}) %all-reduce.2.cloned.1.call-update) | async-done | bytes 262160 | tf_op jit(solution)/shard_map/psum | solution.py:164
  346.0 15.6 %copy.82 = f32[2,17,2,8192]{1,2,0,3:T(2,128)} copy(f32[2,17,2,8192]{3,2,1,0:T(2,128)S(1)} %pad_maximum_fusion.2) | data formatting | bytes 4456448 | tf_op jit(solution)/shard_map/stack | solution.py:26
  361.6 30.5 %reshape.645 = f32[4,1,139264]{2,1,0:T(1,128)} reshape(f32[8192,2,2,17]{3,2,1,0:T(2,128)} %bitcast.192) | data formatting | bytes 4456448
  392.1 4.5 all-to-all-start.2
  396.7 24.8 %all-to-all-done.2 = f32[4,1,139264]{2,1,0:T(1,128)} async-done(((f32[4,1,139264]{2,1,0:T(1,128)}), f32[4,1,139264]{2,1,0:T(1,128)}, u32[]{:S(2)}, u32[]{:S(2)}) %all-to-all-start.2) | async-done | bytes 2228256 | tf_op jit(solution)/shard_map/all_to_all | solution.py:174
  421.5 8.1 %reduce.1 = f32[4,139264]{1,0:T(4,128)S(1)} reduce(f32[4,1,139264]{2,1,0:T(1,128)} %all-to-all-done.2, f32[]{:T(128)} %broadcast.1003), dimensions={1}, to_apply=%all_to_all.45.reduce_sub_computation | reduce | bytes 4456452 | tf_op jit(solution)/shard_map/all_to_all | solution.py:174
  429.6 33.1 %reshape.646 = f32[8192,2,2,17]{3,2,1,0:T(2,128)} reshape(f32[4,139264]{1,0:T(4,128)S(1)} %reduce.1) | data formatting | bytes 4456448
  462.7 20.6 %copy.83 = f32[2,17,2,4,2048]{4,2,3,0,1:T(2,128)S(1)} copy(f32[2,17,2,4,2048]{1,2,0,4,3:T(2,128)} %bitcast.193) | data formatting | bytes 4456448 | tf_op jit(solution)/shard_map/all_to_all | solution.py:174
  485.9 3.8 convolution_bitcast_fusion.1
  490.5 16.9 %all_to_all.54 = f32[2,17,4,2048]{3,0,1,2:T(2,128)S(1)} all-to-all(f32[2,17,4,2048]{3,0,1,2:T(2,128)S(1)} %copy.84), channel_id=1, replica_groups=mesh['chan'=8,'ctx'=4] {'ctx'}, dimensions={2} | all-to-all | bytes 2228224 | tf_op jit(solution)/shard_map/all_to_all | solution.py:178
  (83 shorter events, 74.9 us)
Async XLA Ops:
  35.1 30.9 %all-to-all-start = ((f32[4,1,135168]{2,1,0:T(1,128)}), f32[4,1,135168]{2,1,0:T(1,128)S(1)}, u32[]{:S(2)}, u32[]{:S(2)}) async-start(f32[4,1,135168]{2,1,0:T(1,128)} %reshape.643), calls=%async_computation | async-start | bytes 4325376 | tf_op jit(solution)/shard_map/all_to_all | solution.py:127
  66.1 1.4 copy-start.4
  113.4 53.2 %all-to-all-start.1 = ((f32[2,33,8,2048]{3,0,1,2:T(2,128)}), f32[2,33,8,2048]{3,0,1,2:T(2,128)}, u32[]{:S(2)}, u32[]{:S(2)}) async-start(f32[2,33,8,2048]{3,0,1,2:T(2,128)} %copy.76), calls=%async_computation.1 | async-start | bytes 8650752 | tf_op jit(solution)/shard_map/all_to_all | solution.py:129
  118.3 207.1 %all-reduce.2.cloned.1.call-start = ((), (), s32[]{:S(2)}) async-start(), calls=%async_computation.4 | async-start | bytes 524288 | tf_op jit(solution)/shard_map/psum | solution.py:164
  189.5 4.0 copy-start
  212.5 2.7 copy-start.1
  241.9 2.9 copy-start.3
  244.8 5.2 %copy-start.2 = (f32[33,2,32,256]{3,2,1,0:T(8,128)S(1)}, f32[33,2,32,256]{3,2,1,0:T(8,128)}, u32[]{:S(2)}) copy-start(f32[33,2,32,256]{3,2,1,0:T(8,128)} %copy-done.1) | copy-start | bytes 6488068
  257.3 1.9 copy-start.5
  257.3 3.0 copy-start.6
  392.1 29.4 %all-to-all-start.2 = ((f32[4,1,139264]{2,1,0:T(1,128)}), f32[4,1,139264]{2,1,0:T(1,128)}, u32[]{:S(2)}, u32[]{:S(2)}) async-start(f32[4,1,139264]{2,1,0:T(1,128)} %reshape.645), calls=%async_computation.2 | async-start | bytes 4456448 | tf_op jit(solution)/shard_map/all_to_all | solution.py:174
Sparse Core Ops, SparseCore 0:
  269.5 55.8 all-reduce.1
where the time goes:
time: 524 us; the launch traced here: 518 us
  local copies, waits for them, and re-layouts  219 us (42%)
  waiting for transfers between devices  151 us (29%)
  other arithmetic  57 us (11%)
  matrix products  44.5 us (8%)
  blocking collectives  16.9 us (3%)
  between operations  15 us (3%)
  starting transfers between devices  14.8 us (3%)
    unnamed x21, local copies, waits for them, and re-layouts  102 us
    psum x1, waiting for transfers between devices, local(): filter_part = lax.psum(filter_part, 'chan')  54.3 us
    all_to_all x1, waiting for transfers between devices, local(): lax.all_to_all(mixed_part, 'ctx', split_axis=2, concat_axis=3, tiled=True)  46 us
    all_to_all x1, waiting for transfers between devices, local(): lax.all_to_all(packed, 'ctx', split_axis=3, concat_axis=2, tiled=True)  25.4 us
    all_to_all x1, waiting for transfers between devices, local(): lax.all_to_all(values, 'ctx', split_axis=3, concat_axis=2, tiled=True)  24.8 us
    all_to_all x2, local copies, waits for them, and re-layouts, local(): lax.all_to_all(values, 'ctx', split_axis=3, concat_axis=2, tiled=True)  23.2 us
    all_to_all x1, blocking collectives, local(): lax.all_to_all(restored, 'ctx', split_axis=2, concat_axis=3, tiled=True)  16.9 us
    slice x4, local copies, waits for them, and re-layouts, rotate(): real_part = values[0] * cosine - values[1] * sine_part  16.7 us
  transfers between devices with their start and end apart: 4, of which 4 were waited for; matrix products, arithmetic and copies ran while one was open for 1% of the time, Pallas kernels for 0%

commit v1 on v0

v1 whole, which is shorter than its diff:
```python
import functools
import math

import jax
import jax.numpy as jnp
import numpy as np
from jax import lax
from jax.experimental import pallas as pl
from jax.experimental.pallas import tpu as pltpu
from jax.sharding import PartitionSpec as P

LANES = 256
TILE = 128
F32 = jnp.float32
BF16 = jnp.bfloat16


def split_table(table):
    high = table.astype(np.float32).astype(BF16)
    low = (table - high.astype(np.float64)).astype(np.float32).astype(BF16)
    return high, low


def tables(n1, n2):
    length = n1 * n2
    a = np.arange(n1, dtype=np.int64)
    b = np.arange(n2, dtype=np.int64)
    theta = 2.0 * np.pi / (4 * n1) * (np.outer(4 * a + 1, a) % (4 * n1))
    cosine, sine = np.cos(theta), np.sin(theta)
    high, low = split_table(np.concatenate([cosine, -sine], axis=0))
    first = np.concatenate([high, high, low], axis=1)
    high, low = split_table(np.concatenate([cosine.T, sine.T], axis=1) / length)
    last = np.concatenate([high, high, low], axis=1)
    turn = 2.0 * np.pi / (4 * length) * (np.outer(4 * a + 1, b) % (4 * length))
    turn_re = np.cos(turn).astype(np.float32)
    turn_im = (-np.sin(turn)).astype(np.float32)
    phi = 2.0 * np.pi / n2 * (np.outer(b, b) % n2)
    re, im = np.cos(phi), -np.sin(phi)
    mid_high, mid_low = split_table(np.block([[re, im], [-im, re]]))
    return first, last, turn_re, turn_im, mid_high, mid_low


def split(x):
    high = x.astype(BF16)
    return high, (x - high.astype(F32)).astype(BF16)


def dot(a, b):
    return jnp.dot(a, b, preferred_element_type=F32)


def body(
    d_n, c_n, rows, n1, n2, piece, norm,
    og_hbm, sv_hbm, fl_hbm, first_ref, last_ref, tr_ref, ti_ref, mh_ref, ml_ref,
    ig_out, fg_out,
    og_buf, sv_buf, fl_buf, g_spec, h_spec, p_spec, ig_send, fp_send, fp_recv, rs_send, rs_recv, ag_send,
    loc_sem, send_sem, recv_sem, csend_sem, crecv_sem,
):
    me = lax.axis_index("ctx")
    mc = lax.axis_index("chan")
    chunk = n1 // d_n
    halves = n2 // TILE
    block = chunk * halves * rows
    both = 2 if n1 <= 128 else 1
    ahead = [lax.rem(me + o, d_n) for o in range(d_n)]
    behind = [lax.rem(me + d_n - o, d_n) for o in range(d_n)]
    cahead = [lax.rem(mc + o, c_n) for o in range(c_n)]
    cbehind = [lax.rem(mc + c_n - o, c_n) for o in range(c_n)]

    barrier = pltpu.get_barrier_semaphore()
    for o in range(1, d_n):
        pl.semaphore_signal(barrier, inc=1, device_id={"ctx": ahead[o]}, device_id_type=pl.DeviceIdType.MESH)
    for o in range(1, c_n):
        pl.semaphore_signal(barrier, inc=1, device_id={"chan": cahead[o]}, device_id_type=pl.DeviceIdType.MESH)

    def at_rows(ref, index):
        return ref.at[pl.ds(pl.multiple_of(index * block, block), block), :]

    def at_chunk(ref, index):
        return ref.at[:, pl.ds(pl.multiple_of(index * chunk, chunk), chunk), :]

    locals_ = [
        pltpu.make_async_copy(fl_hbm, at_chunk(fl_buf, me), loc_sem.at[0]),
        pltpu.make_async_copy(og_hbm.at[me], at_rows(og_buf, me), loc_sem.at[1]),
        pltpu.make_async_copy(sv_hbm.at[me], at_rows(sv_buf, me), loc_sem.at[2]),
    ]
    for copy in locals_:
        copy.start()
    pl.semaphore_wait(barrier, d_n + c_n - 2)

    def push(kind, o, src, dst):
        return pltpu.make_async_remote_copy(
            src_ref=src, dst_ref=dst, send_sem=send_sem.at[kind, o], recv_sem=recv_sem.at[kind, o],
            device_id={"ctx": ahead[o]}, device_id_type=pl.DeviceIdType.MESH)

    def cpush(kind, o, src, dst):
        return pltpu.make_async_remote_copy(
            src_ref=src, dst_ref=dst, send_sem=csend_sem.at[kind, o], recv_sem=crecv_sem.at[kind, o],
            device_id={"chan": cahead[o]}, device_id_type=pl.DeviceIdType.MESH)

    peers = range(1, d_n)
    sent = []
    for o in peers:
        sent.append(push(0, o, fl_hbm, at_chunk(fl_buf, me)))
    for o in peers:
        sent.append(push(1, o, og_hbm.at[ahead[o]], at_rows(og_buf, me)))
    for o in peers:
        sent.append(push(2, o, sv_hbm.at[ahead[o]], at_rows(sv_buf, me)))
    for copy in sent:
        copy.start()

    def first_stage(x):
        high, low = split(x)
        out = dot(first_ref[...], jnp.concatenate([high, low, high], axis=0))
        return turned(out[:n1], out[n1:])

    def turned(re, im):
        tr, ti = tr_ref[...], ti_ref[...]
        return jnp.concatenate([re * tr - im * ti, re * ti + im * tr], axis=1)

    def mid_stage(x):
        high, low = split(x)
        return dot(high, mh_ref[...]) + dot(low, mh_ref[...]) + dot(high, ml_ref[...])

    def last_stage(x):
        x = turned(x[:, :n2], x[:, n2:])
        high, low = split(jnp.concatenate([x[:, :n2], x[:, n2:]], axis=0))
        return dot(last_ref[...], jnp.concatenate([high, low, high], axis=0))

    def stacked(parts):
        return parts[0] if len(parts) == 1 else jnp.concatenate(parts, axis=0)

    def row_of(ref, r):
        parts = [ref[pl.ds(h * rows + r, n1, stride=halves * rows), :] for h in range(halves)]
        return jnp.concatenate(parts, axis=1)

    def spectra(ref, i):
        return mid_stage(stacked([first_stage(row_of(ref, i * both + j)) for j in range(both)]))

    def group_rows(i):
        return pl.ds(pl.multiple_of(lax.rem(i * both, 2) * n1, n1), both * n1)

    def span(i):
        return pl.ds(pl.multiple_of(i * (both * n1), both * n1), both * n1)

    locals_[0].wait()
    for o in peers:
        push(0, o, fl_hbm, at_chunk(fl_buf, behind[o])).wait_recv()
    for g in range(0, 2, both):
        h_spec[g * n1 : (g + both) * n1, :] = mid_stage(
            stacked([first_stage(fl_buf[g + j]) for j in range(both)]))

    locals_[1].wait()
    for o in peers:
        push(1, o, og_hbm.at[ahead[o]], at_rows(og_buf, behind[o])).wait_recv()

    def input_step(i, carry):
        grad = spectra(og_buf, i)
        g_spec[span(i), :] = grad
        filt = h_spec[group_rows(i), :]
        gr, gi, hr, hi = grad[:, :n2], grad[:, n2:], filt[:, :n2], filt[:, n2:]
        back = mid_stage(jnp.concatenate([hr * gr + hi * gi, hi * gr - hr * gi], axis=1))
        for j in range(both):
            out = last_stage(back[j * n1 : (j + 1) * n1])
            for h in range(halves):
                ig_send[pl.ds(h * rows + i * both + j, n1, stride=halves * rows), :] = out[:, h * TILE : (h + 1) * TILE]
        return carry

    lax.fori_loop(0, rows // both, input_step, 0)
    own = pltpu.make_async_copy(at_rows(ig_send, me), ig_out.at[me], loc_sem.at[3])
    own.start()
    for o in peers:
        copy = push(3, o, at_rows(ig_send, ahead[o]), ig_out.at[me])
        copy.start()
        sent.append(copy)

    locals_[2].wait()
    for o in peers:
        push(2, o, sv_hbm.at[ahead[o]], at_rows(sv_buf, behind[o])).wait_recv()
    p_spec[...] = jnp.zeros_like(p_spec)

    def filter_step(i, carry):
        spec = spectra(sv_buf, i)
        grad = g_spec[span(i), :]
        xr, xi, gr, gi = spec[:, :n2], spec[:, n2:], grad[:, :n2], grad[:, n2:]
        p_spec[group_rows(i), :] += jnp.concatenate([xr * gr + xi * gi, xi * gr - xr * gi], axis=1)
        return carry

    lax.fori_loop(0, rows // both, filter_step, 0)
    total = mid_stage(p_spec[...])
    for g in range(2):
        part = last_stage(total[g * n1 : (g + 1) * n1])
        per_chunk = chunk // piece
        for d in range(d_n):
            for p in range(per_chunk):
                start = d * chunk + p * piece
                fp_send[d, g * per_chunk + p] = part[start : start + piece, :]

    for o in peers:
        copy = push(4, o, fp_send.at[ahead[o]], fp_recv.at[me])
        copy.start()
        sent.append(copy)
    for o in peers:
        push(4, o, fp_send.at[ahead[o]], fp_recv.at[behind[o]]).wait_recv()
    acc = fp_send[me]
    for o in peers:
        acc = acc + fp_recv[behind[o]]
    rs_send[...] = acc
    for o in range(1, c_n):
        copy = cpush(0, o, rs_send.at[cahead[o]], rs_recv.at[mc])
        copy.start()
        sent.append(copy)
    for o in range(1, c_n):
        cpush(0, o, rs_send.at[cahead[o]], rs_recv.at[cbehind[o]]).wait_recv()
    acc = rs_send[mc]
    for o in range(1, c_n):
        acc = acc + rs_recv[cbehind[o]]
    acc = acc * norm
    ag_send[...] = acc
    fg_out[mc] = acc
    for o in range(1, c_n):
        copy = cpush(1, o, ag_send, fg_out.at[mc])
        copy.start()
        sent.append(copy)
    for o in range(1, c_n):
        cpush(1, o, ag_send, fg_out.at[cbehind[o]]).wait_recv()
    for o in peers:
        push(3, o, at_rows(ig_send, ahead[o]), ig_out.at[behind[o]]).wait_recv()
    own.wait()
    for copy in sent:
        copy.wait_send()


def local(saved_input, out_grad, filters):
    batch, channels, tokens = saved_input.shape
    groups = filters.shape[0]
    d_n, c_n = lax.axis_size("ctx"), lax.axis_size("chan")
    rows = batch * channels // d_n
    n2 = LANES
    chunk = tokens // n2
    n1 = chunk * d_n
    block = chunk * rows * (n2 // TILE)
    piece = groups * chunk // c_n
    assert groups == 2 and rows % 2 == 0 and channels % 2 == 0 and chunk % piece == 0
    norm = float(tokens * d_n * batch * (channels // groups) * c_n) ** -0.5

    def blocks(x):
        return x.reshape(d_n, rows, tokens // TILE, TILE).transpose(0, 2, 1, 3).reshape(d_n, block, TILE)

    first, last, turn_re, turn_im, mid_high, mid_low = tables(n1, n2)
    any_spec = pl.BlockSpec(memory_space=pl.ANY)
    vmem = pl.BlockSpec(memory_space=pltpu.VMEM)
    dma = pltpu.SemaphoreType.DMA
    input_grad, filter_grad = pl.pallas_call(
        functools.partial(body, d_n, c_n, rows, n1, n2, piece, norm),
        out_shape=[
            jax.ShapeDtypeStruct((d_n, block, TILE), F32),
            jax.ShapeDtypeStruct((c_n, piece, n2), F32),
        ],
        in_specs=[any_spec] * 3 + [vmem] * 6,
        out_specs=[any_spec, vmem],
        scratch_shapes=[
            pltpu.VMEM((d_n * block, TILE), F32),
            pltpu.VMEM((d_n * block, TILE), F32),
            pltpu.VMEM((2, n1, n2), F32),
            pltpu.VMEM((rows * n1, 2 * n2), F32),
            pltpu.VMEM((2 * n1, 2 * n2), F32),
            pltpu.VMEM((2 * n1, 2 * n2), F32),
            pltpu.VMEM((d_n * block, TILE), F32),
            pltpu.VMEM((d_n, c_n, piece, n2), F32),
            pltpu.VMEM((d_n, c_n, piece, n2), F32),
            pltpu.VMEM((c_n, piece, n2), F32),
            pltpu.VMEM((c_n, piece, n2), F32),
            pltpu.VMEM((piece, n2), F32),
            dma((4,)),
            dma((5, d_n)),
            dma((5, d_n)),
            dma((2, c_n)),
            dma((2, c_n)),
        ],
        compiler_params=pltpu.CompilerParams(
            collective_id=0, has_side_effects=True, vmem_limit_bytes=48 * 1024 * 1024),
        name="conv_backward",
    )(
        blocks(out_grad), blocks(saved_input), filters.reshape(groups, chunk, n2),
        jnp.asarray(first), jnp.asarray(last), jnp.asarray(turn_re), jnp.asarray(turn_im),
        jnp.asarray(mid_high), jnp.asarray(mid_low),
    )
    input_grad = input_grad.reshape(d_n, tokens // TILE, rows, TILE).transpose(0, 2, 1, 3)
    input_grad = input_grad.reshape(batch, channels, tokens).astype(BF16)
    return input_grad, filter_grad.reshape(groups, tokens)


def solution(mesh):
    placed = (P(None, "chan", "ctx"), P(None, "chan", "ctx"), P(None, "ctx"))
    return jax.shard_map(
        local,
        mesh=mesh,
        in_specs=placed,
        out_specs=(P(None, "chan", "ctx"), P(None, "ctx")),
        check_vma=False,
    )
```

time: 524 us -> 66 us (0.13); the launches traced: 518 us -> 65.7 us
  local copies, waits for them, and re-layouts: 219 us -> 8.89 us
  waiting for transfers between devices: 151 us -> 0 us
  other arithmetic: 57 us -> 0.86 us
  Pallas kernels: 0 us -> 55.3 us
  matrix products: 44.5 us -> 0 us
  blocking collectives: 16.9 us -> 0 us
  starting transfers between devices: 14.8 us -> 0 us
  between operations: 15 us -> 0.65 us
    all_to_all x3 -> x0, waiting for transfers between devices: 96.2 us -> none  [the longest x1 46 us: local(): lax.all_to_all(mixed_part, 'ctx', split_axis=2, concat_axis=3, tiled=True)]
    unnamed x21 -> x17, local copies, waits for them, and re-layouts: 102 us -> 8.22 us
    pallas_call x0 -> x1, Pallas kernels: none -> 55.3 us  [local(): pl.pallas_call(functools.partial(body, d_n, c_n, rows, n1, n2, piece, nor...]
    psum x1 -> x0, waiting for transfers between devices: 54.3 us -> none  [local(): filter_part = lax.psum(filter_part, 'chan')]
    dot_general x18 -> x0, matrix products: 44.5 us -> none  [the longest x4 10.5 us: complex_apply(): jnp.einsum(form, real_part, cosine, precision=precise)]
    all_to_all x4 -> x0, local copies, waits for them, and re-layouts: 34.3 us -> none  [the longest x2 23.2 us: local(): lax.all_to_all(values, 'ctx', split_axis=3, concat_axis=2, tiled=True)]
    slice x13 -> x0, local copies, waits for them, and re-layouts: 33.5 us -> none  [the longest x4 16.7 us: rotate(): real_part = values[0] * cosine - values[1] * sine_part]
    another operation x12 -> x0, other arithmetic: 18.8 us -> none  [the longest x1 6.41 us: local(): jnp.stack([(values[1] + mirror[1]) * 0.5, (mirror[0] - values[0]) * 0.5])]
  transfers between devices with their start and end apart: 4 -> 0, of which waited for: 4 -> 0; matrix products, arithmetic and copies ran while one was open for 1% -> 0% of each run, Pallas kernels for 0% -> 0%
where the time goes in v1:
time: 66 us; the launch traced here: 65.7 us
  Pallas kernels  55.3 us (84%)
  local copies, waits for them, and re-layouts  8.89 us (13%)
  other arithmetic  0.86 us (1%)
    pallas_call x1, Pallas kernels, local(): pl.pallas_call(functools.partial(body, d_n, c_n, rows, n1, n2, piece, nor...  55.3 us
    unnamed x17, local copies, waits for them, and re-layouts  8.22 us

profile of v1, /device:TPU:0, one launch (start us, length us, event | category | flops | bytes accessed | tf_op | source)
XLA Modules:
  0.0 65.7 jit_solution(4964349641461384689)
XLA Ops:
  0.6 0.0 copy-start.6
  0.6 0.9 %copy.13 = f32[1,2,32,256]{3,2,1,0:T(8,128)S(1)} copy(f32[1,2,32,256]{3,1,2,0:T(2,128)} %bitcast.23) | data formatting | bytes 131072
  1.5 0.0 copy-done.6
  1.6 0.0 copy-start
  1.6 1.2 %copy-done = f32[2,16,8192]{2,1,0:T(8,128)S(1)} copy-done((f32[2,16,8192]{2,1,0:T(8,128)S(1)}, f32[2,16,8192]{2,1,0:T(8,128)}, u32[]{:S(2)}) %copy-start) | copy-done | bytes 1048600
  2.8 0.0 copy-start.1
  2.8 1.2 %copy-done.1 = f32[2,16,8192]{2,1,0:T(8,128)S(1)} copy-done((f32[2,16,8192]{2,1,0:T(8,128)S(1)}, f32[2,16,8192]{2,1,0:T(8,128)}, u32[]{:S(2)}) %copy-start.1) | copy-done | bytes 1048600
  4.0 0.0 copy-start.2
  4.0 1.0 %copy-done.2 = bf16[512,512]{1,0:T(8,128)(2,1)S(1)} copy-done((bf16[512,512]{1,0:T(8,128)(2,1)S(1)}, bf16[512,512]{1,0:T(8,128)(2,1)}, u32[]{:S(2)}) %copy-start.2) | copy-done | bytes 524312
  5.1 0.0 copy-start.3
  5.1 1.0 %copy-done.3 = bf16[512,512]{1,0:T(8,128)(2,1)S(1)} copy-done((bf16[512,512]{1,0:T(8,128)(2,1)S(1)}, bf16[512,512]{1,0:T(8,128)(2,1)}, u32[]{:S(2)}) %copy-start.3) | copy-done | bytes 524312
  6.1 0.0 copy-start.4
  6.1 0.9 %copy-done.4 = bf16[128,768]{1,0:T(8,128)(2,1)S(1)} copy-done((bf16[128,768]{1,0:T(8,128)(2,1)S(1)}, bf16[128,768]{1,0:T(8,128)(2,1)}, u32[]{:S(2)}) %copy-start.4) | copy-done | bytes 196632
  7.0 0.0 copy-start.5
  7.0 0.9 %copy-done.5 = bf16[256,384]{1,0:T(8,128)(2,1)S(1)} copy-done((bf16[256,384]{1,0:T(8,128)(2,1)S(1)}, bf16[256,384]{1,0:T(8,128)(2,1)}, u32[]{:S(2)}) %copy-start.5) | copy-done | bytes 196632
  8.0 0.0 copy-start.7
  8.0 0.9 %copy-done.7 = f32[128,256]{1,0:T(8,128)S(1)} copy-done((f32[128,256]{1,0:T(8,128)S(1)}, f32[128,256]{1,0:T(8,128)}, u32[]{:S(2)}) %copy-start.7) | copy-done | bytes 131096
  8.9 55.3 %conv_backward.1 = (f32[4,512,128]{2,1,0:T(8,128)S(1)}, f32[8,8,256]{2,1,0:T(8,128)S(1)}) custom-call(f32[4,512,128]{2,1,0:T(8,128)S(1)} %bitcast.19, f32[4,512,128]{2,1,0:T(8,128)S(1)} %bitcast.20, f32[2,32,256]{2,1,0:T(8,128)S(1)} %bitcast.21, bf16[256,384]{1,0:T(8,128)(2,1)S(1)} %copy-done.5, bf16[128,768]{1,0:T(8,128)(2,1)S(1)} %copy-done.4, ...), custom_call_target="tpu_custom_call" | custom-call | tf_op jit(solution)/shard_map/conv_backward/pallas_call | solution.py:254
  64.1 0.9 %convert_element_type.12 = bf16[4,512,128]{2,1,0:T(8,128)(2,1)} convert(f32[4,512,128]{2,1,0:T(8,128)S(1)} %get-tuple-element.4) | non-fusion elementwise | flops 262144 | bytes 1572864 | tf_op jit(solution)/shard_map/convert_element_type | solution.py:290
  65.0 0.7 %reshape.31 = f32[2,8192]{1,0:T(2,128)} reshape(f32[8,8,256]{2,1,0:T(8,128)S(1)} %get-tuple-element.5) | data formatting | bytes 131072 | tf_op jit(solution)/shard_map/reshape | solution.py:291
Async XLA Ops:
  0.6 0.9 %copy-start.6 = (f32[128,256]{1,0:T(8,128)S(1)}, f32[128,256]{1,0:T(8,128)}, u32[]{:S(2)}) copy-start(f32[128,256]{1,0:T(8,128)} %constant.15.clone.ti_ref) | copy-start | bytes 393220
  1.6 1.2 %copy-start = (f32[2,16,8192]{2,1,0:T(8,128)S(1)}, f32[2,16,8192]{2,1,0:T(8,128)}, u32[]{:S(2)}) copy-start(f32[2,16,8192]{2,1,0:T(8,128)} %param.10) | copy-start | bytes 3145732
  2.8 1.2 %copy-start.1 = (f32[2,16,8192]{2,1,0:T(8,128)S(1)}, f32[2,16,8192]{2,1,0:T(8,128)}, u32[]{:S(2)}) copy-start(f32[2,16,8192]{2,1,0:T(8,128)} %param.9) | copy-start | bytes 3145732
  4.0 1.0 %copy-start.2 = (bf16[512,512]{1,0:T(8,128)(2,1)S(1)}, bf16[512,512]{1,0:T(8,128)(2,1)}, u32[]{:S(2)}) copy-start(bf16[512,512]{1,0:T(8,128)(2,1)} %constant.17.clone.ml_ref) | copy-start | bytes 1572868
  5.1 1.0 %copy-start.3 = (bf16[512,512]{1,0:T(8,128)(2,1)S(1)}, bf16[512,512]{1,0:T(8,128)(2,1)}, u32[]{:S(2)}) copy-start(bf16[512,512]{1,0:T(8,128)(2,1)} %constant.16.clone.mh_ref) | copy-start | bytes 1572868
  6.1 0.9 %copy-start.4 = (bf16[128,768]{1,0:T(8,128)(2,1)S(1)}, bf16[128,768]{1,0:T(8,128)(2,1)}, u32[]{:S(2)}) copy-start(bf16[128,768]{1,0:T(8,128)(2,1)} %constant.13.clone.last_ref) | copy-start | bytes 589828
  7.0 0.9 %copy-start.5 = (bf16[256,384]{1,0:T(8,128)(2,1)S(1)}, bf16[256,384]{1,0:T(8,128)(2,1)}, u32[]{:S(2)}) copy-start(bf16[256,384]{1,0:T(8,128)(2,1)} %constant.12.clone.first_ref) | copy-start | bytes 589828
  8.0 0.9 %copy-start.7 = (f32[128,256]{1,0:T(8,128)S(1)}, f32[128,256]{1,0:T(8,128)}, u32[]{:S(2)}) copy-start(f32[128,256]{1,0:T(8,128)} %constant.14.clone.tr_ref) | copy-start | bytes 393220

commit v2 on v1

--- a/solution.py
+++ b/solution.py
@@ -50,17 +50,19 @@
 
 
 def body(
-    d_n, c_n, rows, n1, n2, piece, norm,
-    og_hbm, sv_hbm, fl_hbm, first_ref, last_ref, tr_ref, ti_ref, mh_ref, ml_ref,
+    d_n, c_n, rows, n1, n2, piece,
+    og_hbm, sv_hbm, fl_hbm, first_hbm, last_hbm, tr_hbm, ti_hbm, mh_hbm, ml_hbm,
     ig_out, fg_out,
     og_buf, sv_buf, fl_buf, g_spec, h_spec, p_spec, ig_send, fp_send, fp_recv, rs_send, rs_recv, ag_send,
-    loc_sem, send_sem, recv_sem, csend_sem, crecv_sem,
+    first_ref, last_ref, tr_ref, ti_ref, mh_ref, ml_ref,
+    loc_sem, tab_sem, send_sem, recv_sem, csend_sem, crecv_sem,
 ):
     me = lax.axis_index("ctx")
     mc = lax.axis_index("chan")
     chunk = n1 // d_n
     halves = n2 // TILE
     block = chunk * halves * rows
+    fblock = chunk * halves * 2
     both = 2 if n1 <= 128 else 1
     ahead = [lax.rem(me + o, d_n) for o in range(d_n)]
     behind = [lax.rem(me + d_n - o, d_n) for o in range(d_n)]
@@ -76,15 +78,26 @@
     def at_rows(ref, index):
         return ref.at[pl.ds(pl.multiple_of(index * block, block), block), :]
 
-    def at_chunk(ref, index):
-        return ref.at[:, pl.ds(pl.multiple_of(index * chunk, chunk), chunk), :]
-
+    def at_filters(ref, index):
+        return ref.at[pl.ds(pl.multiple_of(index * fblock, fblock), fblock), :]
+
+    def at_half(ref, index, half):
+        return ref.at[pl.ds(pl.multiple_of(index * block + half * (block // 2), block // 2), block // 2), :]
+
+    def at_piece(ref, index):
+        return ref.at[pl.ds(pl.multiple_of(index * piece, piece), piece), :]
+
+    loads = [
+        pltpu.make_async_copy(src, dst, tab_sem.at[index])
+        for index, (src, dst) in enumerate(
+            [(first_hbm, first_ref), (last_hbm, last_ref), (tr_hbm, tr_ref), (ti_hbm, ti_ref), (mh_hbm, mh_ref), (ml_hbm, ml_ref)])
+    ]
     locals_ = [
-        pltpu.make_async_copy(fl_hbm, at_chunk(fl_buf, me), loc_sem.at[0]),
+        pltpu.make_async_copy(fl_hbm, at_filters(fl_buf, me), loc_sem.at[0]),
         pltpu.make_async_copy(og_hbm.at[me], at_rows(og_buf, me), loc_sem.at[1]),
         pltpu.make_async_copy(sv_hbm.at[me], at_rows(sv_buf, me), loc_sem.at[2]),
     ]
-    for copy in locals_:
+    for copy in loads + locals_:
         copy.start()
     pl.semaphore_wait(barrier, d_n + c_n - 2)
 
@@ -101,7 +114,7 @@
     peers = range(1, d_n)
     sent = []
     for o in peers:
-        sent.append(push(0, o, fl_hbm, at_chunk(fl_buf, me)))
+        sent.append(push(0, o, fl_hbm, at_filters(fl_buf, me)))
     for o in peers:
         sent.append(push(1, o, og_hbm.at[ahead[o]], at_rows(og_buf, me)))
     for o in peers:
@@ -130,7 +143,7 @@
     def stacked(parts):
         return parts[0] if len(parts) == 1 else jnp.concatenate(parts, axis=0)
 
-    def row_of(ref, r):
+    def row_of(ref, r, rows=rows):
         parts = [ref[pl.ds(h * rows + r, n1, stride=halves * rows), :] for h in range(halves)]
         return jnp.concatenate(parts, axis=1)
 
@@ -143,12 +156,14 @@
     def span(i):
         return pl.ds(pl.multiple_of(i * (both * n1), both * n1), both * n1)
 
+    for copy in loads:
+        copy.wait()
     locals_[0].wait()
     for o in peers:
-        push(0, o, fl_hbm, at_chunk(fl_buf, behind[o])).wait_recv()
+        push(0, o, fl_hbm, at_filters(fl_buf, behind[o])).wait_recv()
     for g in range(0, 2, both):
         h_spec[g * n1 : (g + both) * n1, :] = mid_stage(
-            stacked([first_stage(fl_buf[g + j]) for j in range(both)]))
+            stacked([first_stage(row_of(fl_buf, g + j, 2)) for j in range(both)]))
 
     locals_[1].wait()
     for o in peers:
@@ -167,10 +182,10 @@
         return carry
 
     lax.fori_loop(0, rows // both, input_step, 0)
-    own = pltpu.make_async_copy(at_rows(ig_send, me), ig_out.at[me], loc_sem.at[3])
+    own = pltpu.make_async_copy(at_rows(ig_send, me), at_rows(ig_out, me), loc_sem.at[3])
     own.start()
     for o in peers:
-        copy = push(3, o, at_rows(ig_send, ahead[o]), ig_out.at[me])
+        copy = push(3, o, at_half(ig_send, ahead[o], 0), at_half(ig_out, me, 0))
         copy.start()
         sent.append(copy)
 
@@ -190,42 +205,43 @@
     total = mid_stage(p_spec[...])
     for g in range(2):
         part = last_stage(total[g * n1 : (g + 1) * n1])
-        per_chunk = chunk // piece
-        for d in range(d_n):
-            for p in range(per_chunk):
-                start = d * chunk + p * piece
-                fp_send[d, g * per_chunk + p] = part[start : start + piece, :]
-
-    for o in peers:
-        copy = push(4, o, fp_send.at[ahead[o]], fp_recv.at[me])
-        copy.start()
-        sent.append(copy)
-    for o in peers:
-        push(4, o, fp_send.at[ahead[o]], fp_recv.at[behind[o]]).wait_recv()
-    acc = fp_send[me]
-    for o in peers:
-        acc = acc + fp_recv[behind[o]]
+        for h in range(halves):
+            fp_send[pl.ds(h * 2 + g, n1, stride=halves * 2), :] = part[:, h * TILE : (h + 1) * TILE]
+
+    for o in peers:
+        copy = push(4, o, at_filters(fp_send, ahead[o]), at_filters(fp_recv, me))
+        copy.start()
+        sent.append(copy)
+    for o in peers:
+        copy = push(5, o, at_half(ig_send, ahead[o], 1), at_half(ig_out, me, 1))
+        copy.start()
+        sent.append(copy)
+    for o in peers:
+        push(4, o, at_filters(fp_send, ahead[o]), at_filters(fp_recv, behind[o])).wait_recv()
+    acc = at_filters(fp_send, me)[...]
+    for o in peers:
+        acc = acc + at_filters(fp_recv, behind[o])[...]
     rs_send[...] = acc
     for o in range(1, c_n):
-        copy = cpush(0, o, rs_send.at[cahead[o]], rs_recv.at[mc])
-        copy.start()
-        sent.append(copy)
-    for o in range(1, c_n):
-        cpush(0, o, rs_send.at[cahead[o]], rs_recv.at[cbehind[o]]).wait_recv()
-    acc = rs_send[mc]
-    for o in range(1, c_n):
-        acc = acc + rs_recv[cbehind[o]]
-    acc = acc * norm
+        copy = cpush(0, o, at_piece(rs_send, cahead[o]), at_piece(rs_recv, mc))
+        copy.start()
+        sent.append(copy)
+    for o in range(1, c_n):
+        cpush(0, o, at_piece(rs_send, cahead[o]), at_piece(rs_recv, cbehind[o])).wait_recv()
+    acc = at_piece(rs_send, mc)[...]
+    for o in range(1, c_n):
+        acc = acc + at_piece(rs_recv, cbehind[o])[...]
     ag_send[...] = acc
-    fg_out[mc] = acc
-    for o in range(1, c_n):
-        copy = cpush(1, o, ag_send, fg_out.at[mc])
-        copy.start()
-        sent.append(copy)
-    for o in range(1, c_n):
-        cpush(1, o, ag_send, fg_out.at[cbehind[o]]).wait_recv()
-    for o in peers:
-        push(3, o, at_rows(ig_send, ahead[o]), ig_out.at[behind[o]]).wait_recv()
+    fg_out[pl.ds(pl.multiple_of(mc * piece, piece), piece), :] = acc
+    for o in range(1, c_n):
+        copy = cpush(1, o, ag_send, at_piece(fg_out, mc))
+        copy.start()
+        sent.append(copy)
+    for o in range(1, c_n):
+        cpush(1, o, ag_send, at_piece(fg_out, cbehind[o])).wait_recv()
+    for half, kind in ((0, 3), (1, 5)):
+        for o in peers:
+            push(kind, o, at_half(ig_send, ahead[o], half), at_half(ig_out, behind[o], half)).wait_recv()
     own.wait()
     for copy in sent:
         copy.wait_send()
@@ -240,55 +256,61 @@
     chunk = tokens // n2
     n1 = chunk * d_n
     block = chunk * rows * (n2 // TILE)
-    piece = groups * chunk // c_n
-    assert groups == 2 and rows % 2 == 0 and channels % 2 == 0 and chunk % piece == 0
+    fblock = groups * tokens // TILE
+    piece = fblock // c_n
+    assert groups == 2 and rows % 2 == 0 and channels % 2 == 0 and piece % 8 == 0
     norm = float(tokens * d_n * batch * (channels // groups) * c_n) ** -0.5
 
     def blocks(x):
         return x.reshape(d_n, rows, tokens // TILE, TILE).transpose(0, 2, 1, 3).reshape(d_n, block, TILE)
 
-    first, last, turn_re, turn_im, mid_high, mid_low = tables(n1, n2)
+    held = tables(n1, n2)
     any_spec = pl.BlockSpec(memory_space=pl.ANY)
     vmem = pl.BlockSpec(memory_space=pltpu.VMEM)
     dma = pltpu.SemaphoreType.DMA
     input_grad, filter_grad = pl.pallas_call(
-        functools.partial(body, d_n, c_n, rows, n1, n2, piece, norm),
+        functools.partial(body, d_n, c_n, rows, n1, n2, piece),
         out_shape=[
-            jax.ShapeDtypeStruct((d_n, block, TILE), F32),
-            jax.ShapeDtypeStruct((c_n, piece, n2), F32),
+            jax.ShapeDtypeStruct((d_n * block, TILE), F32),
+            jax.ShapeDtypeStruct((fblock, TILE), F32),
         ],
-        in_specs=[any_spec] * 3 + [vmem] * 6,
+        in_specs=[any_spec] * 9,
         out_specs=[any_spec, vmem],
         scratch_shapes=[
             pltpu.VMEM((d_n * block, TILE), F32),
             pltpu.VMEM((d_n * block, TILE), F32),
-            pltpu.VMEM((2, n1, n2), F32),
+            pltpu.VMEM((d_n * fblock, TILE), F32),
             pltpu.VMEM((rows * n1, 2 * n2), F32),
             pltpu.VMEM((2 * n1, 2 * n2), F32),
             pltpu.VMEM((2 * n1, 2 * n2), F32),
             pltpu.VMEM((d_n * block, TILE), F32),
-            pltpu.VMEM((d_n, c_n, piece, n2), F32),
-            pltpu.VMEM((d_n, c_n, piece, n2), F32),
-            pltpu.VMEM((c_n, piece, n2), F32),
-            pltpu.VMEM((c_n, piece, n2), F32),
-            pltpu.VMEM((piece, n2), F32),
+            pltpu.VMEM((d_n * fblock, TILE), F32),
+            pltpu.VMEM((d_n * fblock, TILE), F32),
+            pltpu.VMEM((fblock, TILE), F32),
+            pltpu.VMEM((fblock, TILE), F32),
+            pltpu.VMEM((piece, TILE), F32),
+        ]
+        + [pltpu.VMEM(table.shape, table.dtype) for table in held]
+        + [
             dma((4,)),
-            dma((5, d_n)),
-            dma((5, d_n)),
+            dma((len(held),)),
+            dma((6, d_n)),
+            dma((6, d_n)),
             dma((2, c_n)),
             dma((2, c_n)),
         ],
         compiler_params=pltpu.CompilerParams(
-            collective_id=0, has_side_effects=True, vmem_limit_bytes=48 * 1024 * 1024),
+            collective_id=0, has_side_effects=True, vmem_limit_bytes=60 * 1024 * 1024),
         name="conv_backward",
     )(
-        blocks(out_grad), blocks(saved_input), filters.reshape(groups, chunk, n2),
-        jnp.asarray(first), jnp.asarray(last), jnp.asarray(turn_re), jnp.asarray(turn_im),
-        jnp.asarray(mid_high), jnp.asarray(mid_low),
+        blocks(out_grad), blocks(saved_input),
+        filters.reshape(groups, tokens // TILE, TILE).transpose(1, 0, 2).reshape(fblock, TILE),
+        *(jnp.asarray(table) for table in held),
     )
     input_grad = input_grad.reshape(d_n, tokens // TILE, rows, TILE).transpose(0, 2, 1, 3)
     input_grad = input_grad.reshape(batch, channels, tokens).astype(BF16)
-    return input_grad, filter_grad.reshape(groups, tokens)
+    filter_grad = filter_grad.reshape(tokens // TILE, groups, TILE).transpose(1, 0, 2)
+    return input_grad, filter_grad.reshape(groups, tokens) * norm
 
 
 def solution(mesh):

time: 66 us -> 57.9 us (0.88)
  local copies, waits for them, and re-layouts: 8.89 us -> 0.01 us
  other arithmetic: 0.86 us -> 2.74 us
  Pallas kernels: 55.3 us -> 54.3 us
    unnamed x17 -> x2, local copies, waits for them, and re-layouts: 8.22 us -> 0.01 us
    convert_element_type x1, other arithmetic: 0.86 us -> 2.1 us  [local(): input_grad = input_grad.reshape(batch, channels, tokens).astype(BF16)]
    pallas_call x1, Pallas kernels: 55.3 us -> 54.3 us  [local(): pl.pallas_call(functools.partial(body, d_n, c_n, rows, n1, n2, piece), ou...]
    reshape x1 -> x0, local copies, waits for them, and re-layouts: 0.67 us -> none  [local(): return (input_grad, filter_grad.reshape(groups, tokens))]
where the time goes in v2:
time: 57.9 us; the launch traced here: 57.7 us
  Pallas kernels  54.3 us (94%)
  other arithmetic  2.74 us (5%)
  between operations  0.65 us (1%)
    pallas_call x1, Pallas kernels, local(): pl.pallas_call(functools.partial(body, d_n, c_n, rows, n1, n2, piece), ou...  54.3 us
    convert_element_type x1, other arithmetic, local(): input_grad = input_grad.reshape(batch, channels, tokens).astype(BF16)  2.1 us

profile of v2, /device:TPU:0, one launch (start us, length us, event | category | flops | bytes accessed | tf_op | source)
XLA Modules:
  0.0 57.7 jit_solution(10145442500450129597)
XLA Ops:
  0.6 54.3 %conv_backward.1 = (f32[2048,128]{1,0:T(8,128)}, f32[128,128]{1,0:T(8,128)}) custom-call(f32[4,512,128]{2,1,0:T(8,128)} %bitcast.25, f32[4,512,128]{2,1,0:T(8,128)} %bitcast.26, f32[128,128]{1,0:T(8,128)} %bitcast.28, bf16[256,384]{1,0:T(8,128)(2,1)} %constant.14.clone.first_hbm, bf16[128,768]{1,0:T(8,128)(2,1)} %constant.15.clone.last_hbm, ...), custom_call_target="tpu_custom_call" | custom-call | tf_op jit(solution)/shard_map/conv_backward/pallas_call | solution.py:271
  55.0 0.0 copy-start
  55.0 2.1 %convert_element_type.12 = bf16[2048,128]{1,0:T(8,128)(2,1)} convert(f32[2048,128]{1,0:T(8,128)} %get-tuple-element.4) | non-fusion elementwise | flops 262144 | bytes 1572864 | tf_op jit(solution)/shard_map/convert_element_type | solution.py:311
  57.1 0.0 copy-done
  57.1 0.6 %broadcast_multiply_fusion = f32[128,128]{1,0:T(8,128)} fusion(f32[128,128]{1,0:T(8,128)S(1)} %copy-done), kind=kLoop, calls=%fused_computation | loop fusion | flops 16384 | bytes 131072 | tf_op jit(solution)/shard_map/mul | solution.py:313
Async XLA Ops:
  55.0 2.1 %copy-start = (f32[128,128]{1,0:T(8,128)S(1)}, f32[128,128]{1,0:T(8,128)}, u32[]{:S(2)}) copy-start(f32[128,128]{1,0:T(8,128)} %get-tuple-element.5) | copy-start | bytes 196612

commit v3 on v2

--- a/solution.py
+++ b/solution.py
@@ -55,7 +55,7 @@
     ig_out, fg_out,
     og_buf, sv_buf, fl_buf, g_spec, h_spec, p_spec, ig_send, fp_send, fp_recv, rs_send, rs_recv, ag_send,
     first_ref, last_ref, tr_ref, ti_ref, mh_ref, ml_ref,
-    loc_sem, tab_sem, send_sem, recv_sem, csend_sem, crecv_sem,
+    loc_sem, tab_sem, send_sem, recv_sem, csend_sem, crecv_sem, fsend_sem, frecv_sem,
 ):
     me = lax.axis_index("ctx")
     mc = lax.axis_index("chan")
@@ -111,10 +111,20 @@
             src_ref=src, dst_ref=dst, send_sem=csend_sem.at[kind, o], recv_sem=crecv_sem.at[kind, o],
             device_id={"chan": cahead[o]}, device_id_type=pl.DeviceIdType.MESH)
 
+    def filter_piece(chunk_index, piece_index):
+        start = pl.multiple_of(chunk_index * fblock + piece_index * piece, piece)
+        return fl_buf.at[pl.ds(start, piece), :]
+
+    def share(o, q, chunk_index, piece_index):
+        view = filter_piece(chunk_index, piece_index)
+        return pltpu.make_async_remote_copy(
+            src_ref=view, dst_ref=view, send_sem=fsend_sem.at[o, q], recv_sem=frecv_sem.at[o, q],
+            device_id={"chan": cahead[q]}, device_id_type=pl.DeviceIdType.MESH)
+
     peers = range(1, d_n)
     sent = []
     for o in peers:
-        sent.append(push(0, o, fl_hbm, at_filters(fl_buf, me)))
+        sent.append(push(0, o, at_piece(fl_hbm, mc), filter_piece(me, mc)))
     for o in peers:
         sent.append(push(1, o, og_hbm.at[ahead[o]], at_rows(og_buf, me)))
     for o in peers:
@@ -160,7 +170,14 @@
         copy.wait()
     locals_[0].wait()
     for o in peers:
-        push(0, o, fl_hbm, at_filters(fl_buf, behind[o])).wait_recv()
+        push(0, o, at_piece(fl_hbm, mc), filter_piece(behind[o], mc)).wait_recv()
+        for q in range(1, c_n):
+            copy = share(o, q, behind[o], mc)
+            copy.start()
+            sent.append(copy)
+    for o in peers:
+        for q in range(1, c_n):
+            share(o, q, behind[o], cbehind[q]).wait_recv()
     for g in range(0, 2, both):
         h_spec[g * n1 : (g + both) * n1, :] = mid_stage(
             stacked([first_stage(row_of(fl_buf, g + j, 2)) for j in range(both)]))
@@ -265,7 +282,7 @@
         return x.reshape(d_n, rows, tokens // TILE, TILE).transpose(0, 2, 1, 3).reshape(d_n, block, TILE)
 
     held = tables(n1, n2)
-    any_spec = pl.BlockSpec(memory_space=pl.ANY)
+    hbm = pl.BlockSpec(memory_space=pltpu.HBM)
     vmem = pl.BlockSpec(memory_space=pltpu.VMEM)
     dma = pltpu.SemaphoreType.DMA
     input_grad, filter_grad = pl.pallas_call(
@@ -274,8 +291,8 @@
             jax.ShapeDtypeStruct((d_n * block, TILE), F32),
             jax.ShapeDtypeStruct((fblock, TILE), F32),
         ],
-        in_specs=[any_spec] * 9,
-        out_specs=[any_spec, vmem],
+        in_specs=[hbm] * 9,
+        out_specs=[hbm, vmem],
         scratch_shapes=[
             pltpu.VMEM((d_n * block, TILE), F32),
             pltpu.VMEM((d_n * block, TILE), F32),
@@ -298,6 +315,8 @@
             dma((6, d_n)),
             dma((2, c_n)),
             dma((2, c_n)),
+            dma((d_n, c_n)),
+            dma((d_n, c_n)),
         ],
         compiler_params=pltpu.CompilerParams(
             collective_id=0, has_side_effects=True, vmem_limit_bytes=60 * 1024 * 1024),

time: 57.9 us -> 56 us (0.967)
  Pallas kernels: 54.3 us -> 52.5 us
    pallas_call x1, Pallas kernels: 54.3 us -> 52.5 us  [local(): pl.pallas_call(functools.partial(body, d_n, c_n, rows, n1, n2, piece), ou...]
where the time goes in v3:
time: 56 us; the launch traced here: 55.9 us
  Pallas kernels  52.5 us (94%)
  other arithmetic  2.74 us (5%)
  between operations  0.65 us (1%)
    pallas_call x1, Pallas kernels, local(): pl.pallas_call(functools.partial(body, d_n, c_n, rows, n1, n2, piece), ou...  52.5 us
    convert_element_type x1, other arithmetic, local(): input_grad = input_grad.reshape(batch, channels, tokens).astype(BF16)  2.1 us

profile of v3, /device:TPU:0, one launch (start us, length us, event | category | flops | bytes accessed | tf_op | source)
XLA Modules:
  0.0 55.9 jit_solution(3739131886068954431)
XLA Ops:
  0.6 52.5 %conv_backward.1 = (f32[2048,128]{1,0:T(8,128)}, f32[128,128]{1,0:T(8,128)}) custom-call(f32[4,512,128]{2,1,0:T(8,128)} %bitcast.25, f32[4,512,128]{2,1,0:T(8,128)} %bitcast.26, f32[128,128]{1,0:T(8,128)} %bitcast.28, bf16[256,384]{1,0:T(8,128)(2,1)} %constant.14.clone.first_hbm, bf16[128,768]{1,0:T(8,128)(2,1)} %constant.15.clone.last_hbm, ...), custom_call_target="tpu_custom_call" | custom-call | tf_op jit(solution)/shard_map/conv_backward/pallas_call | solution.py:288
  53.1 0.0 copy-start
  53.1 2.1 %convert_element_type.12 = bf16[2048,128]{1,0:T(8,128)(2,1)} convert(f32[2048,128]{1,0:T(8,128)} %get-tuple-element.4) | non-fusion elementwise | flops 262144 | bytes 1572864 | tf_op jit(solution)/shard_map/convert_element_type | solution.py:330
  55.2 0.0 copy-done
  55.2 0.6 %broadcast_multiply_fusion = f32[128,128]{1,0:T(8,128)} fusion(f32[128,128]{1,0:T(8,128)S(1)} %copy-done), kind=kLoop, calls=%fused_computation | loop fusion | flops 16384 | bytes 131072 | tf_op jit(solution)/shard_map/mul | solution.py:332
Async XLA Ops:
  53.1 2.1 %copy-start = (f32[128,128]{1,0:T(8,128)S(1)}, f32[128,128]{1,0:T(8,128)}, u32[]{:S(2)}) copy-start(f32[128,128]{1,0:T(8,128)} %get-tuple-element.5) | copy-start | bytes 196612
